TPU v7x, 128 devices: a whole 4x4x4 slice. The times are simulated.
128 devices in a mesh: past: 8 (over y, z_lo), second: 16 (over x, z_hi, core).
Axes of the slice: x: 4, y: 4, z: 4 (z_hi: 2, z_lo: 2; z = z_hi * 2 + z_lo), core: 2. Of those that a mesh axis runs over, the one named last changes fastest.
Arguments:
- resident: bfloat16 [24576, 24576], P('past', 'second'), may hold values from -6 to 6
- memory: bfloat16 [2, 384, 24576], P(None, None, 'past'), may hold values from -0.0390625 to 0.0390625
- previous: bfloat16 [2, 384, 24576], P(None, None, 'second'), may hold values from -6 to 6
- inverse_part: float32 [2, 384, 384], replicated, may hold values from -0.3125 to 0.3125
- pair_coupling: float32 [32, 32], replicated, may hold values from 0.000318944 to 0.00318944
Outputs:
- fronts: bfloat16 [2, 384, 24576], P(None, None, 'second')
All inputs are finite; a program needn't handle non-finite values.
Results may differ from a plain program's by a relative error of at most 0.017.
Values may be sent and summed in bfloat16 or wider, within the bound.
No kernel may reach another device: no remote copies, remote signals or barrier semaphores. Data moves between devices by JAX's collectives and lax.ppermute only.
A program may use at most 128 MiB of HBM per device.

v0:
```python
import jax
import jax.numpy as jnp
from jax import lax
from jax.sharding import PartitionSpec as P

step_size = 0.5


def orbital_flip(block, orbitals):
    row_count, col_count = block.shape
    blocks = block.reshape(row_count // orbitals, orbitals, col_count // orbitals, orbitals)
    return blocks.transpose(0, 3, 2, 1).reshape(row_count, col_count)


def solve_front(summed, prior, inverse_block):
    source = prior.astype(jnp.float32) - step_size * summed
    solved = source + jnp.dot(
        inverse_block, source, precision=lax.Precision.HIGHEST, preferred_element_type=jnp.float32
    )
    return solved.astype(jnp.bfloat16)


def self_energy(front, pair_coupling):
    orbitals = pair_coupling.shape[0]
    row_count, col_count = front.shape
    values = front.astype(jnp.float32)
    mirror = orbital_flip(values, orbitals)
    blocks = (values * values * mirror).reshape(
        row_count // orbitals, orbitals, col_count // orbitals, orbitals
    )
    return (
        (blocks * pair_coupling[None, :, None, :])
        .reshape(row_count, col_count)
        .astype(jnp.bfloat16)
    )


def per_device(resident, memory, previous, inverse_part, pair_coupling):

    def advance(memory_row, front_index):
        partial_value = jnp.dot(memory_row, resident, preferred_element_type=jnp.float32)
        summed = lax.psum(partial_value.astype(jnp.bfloat16), "past").astype(jnp.float32)
        prior_cols = previous[front_index]
        return solve_front(summed, prior_cols, inverse_part[front_index])

    front_one = advance(memory[0], 0)
    energy_one = self_energy(front_one, pair_coupling)
    span_cols = memory.shape[2]
    whole_row = lax.all_gather(energy_one, "second", axis=1, tiled=True)
    gathered = lax.dynamic_slice_in_dim(whole_row, lax.axis_index("past") * span_cols, span_cols, 1)
    orbitals = pair_coupling.shape[0]
    memory_next = (
        memory[1].astype(jnp.float32) + orbital_flip(gathered, orbitals).astype(jnp.float32)
    ).astype(jnp.bfloat16)
    front_two = advance(memory_next, 1)
    return jnp.stack([front_one, front_two])


def solution(mesh):
    in_specs = (P("past", "second"), P(None, None, "past"), P(None, None, "second"), P(), P())
    out_specs = P(None, None, "second")
    return jax.shard_map(
        per_device, mesh=mesh, in_specs=in_specs, out_specs=out_specs, check_vma=False
    )
```

profile of v0, /device:TPU:0, one launch (start us, length us, event | category | flops | bytes accessed | tf_op | source)
XLA Modules:
  0.0 406.2 jit_solution(5935509110012505917)
XLA Ops:
  6.5 0.0 copy-start
  6.5 0.0 all-reduce.3.cloned.1.call-start
  6.5 9.2 %convolution_convert_fusion.1 = bf16[384,1536]{1,0:T(8,128)(2,1)} fusion(bf16[3072,1536]{1,0:T(8,128)(2,1)} %param.5, bf16[2,384,3072]{2,1,0:T(8,128)(2,1)} %param.6), kind=kOutput, calls=%fused_computation.9 | convolution fusion | flops 3624468480 | bytes 12976128 | tf_op jit(solution)/shard_map/dot_general | solution.py:41
  15.8 0.0 all-reduce.3.cloned.1.call-update
  15.8 0.0 all-gather.2.cloned.1.call-start
  15.8 0.0 copy-done
  15.9 4.4 %mul.29 = f32[12,32,48,32]{3,2,1,0:T(8,128)} broadcast(f32[32,32]{1,0:T(8,128)S(1)} %copy-done), dimensions={1,3} | broadcast | bytes 2363392 | tf_op jit(solution)/shard_map/mul | solution.py:32
  20.3 6.7 %mul.30 = f32[384,1536]{1,0:T(8,128)S(1)} reshape(f32[12,32,48,32]{3,2,1,0:T(8,128)} %mul.29) | data formatting | bytes 4718592 | tf_op jit(solution)/shard_map/mul | solution.py:32
  27.0 70.5 %all-reduce.3.cloned.1.call-done = bf16[384,1536]{1,0:T(8,128)(2,1)} async-done(((bf16[384,1536]{1,0:T(8,128)(2,1)}), bf16[384,1536]{1,0:T(8,128)(2,1)}) %all-reduce.3.cloned.1.call-update) | async-done | bytes 1179664 | tf_op jit(solution)/shard_map/psum | solution.py:42
  97.5 6.8 %fusion.3 = bf16[384,1536]{1,0:T(8,128)(2,1)S(1)} fusion(bf16[384,1536]{1,0:T(8,128)(2,1)} %all-reduce.3.cloned.1.call-done, bf16[2,384,1536]{2,1,0:T(8,128)(2,1)} %param.7, f32[2,384,384]{2,1,0:T(8,128)} %param.8), kind=kOutput, calls=%fused_computation.6 | convolution fusion | flops 2723807232 | bytes 6488064 | tf_op jit(solution)/shard_map/dot_general | solution.py:17
  104.3 4.9 %reshape.22 = f32[12,32,48,32]{3,2,1,0:T(8,128)} reshape(bf16[384,1536]{1,0:T(8,128)(2,1)S(1)} %fusion.3) | data formatting | bytes 3538944 | tf_op jit(solution)/shard_map/reshape | solution.py:11
  109.2 10.8 %copy.11 = f32[12,32,48,32]{3,2,1,0:T(8,128)} copy(f32[12,32,48,32]{1,2,3,0:T(8,128)} %bitcast.55) | data formatting | bytes 4718592 | tf_op jit(solution)/shard_map/transpose | solution.py:12
  120.0 7.7 %reshape.23 = f32[384,1536]{1,0:T(8,128)} reshape(f32[12,32,48,32]{3,2,1,0:T(8,128)} %copy.11) | data formatting | bytes 4718592 | tf_op jit(solution)/shard_map/reshape | solution.py:12
  127.8 3.3 multiply_convert_fusion
  131.1 0.0 all-gather.2.cloned.1.call-update
  131.1 0.2 all-reduce.5.cloned.1.call-start
  131.3 119.3 %all-gather.2.cloned.1.call-done = bf16[384,24576]{1,0:T(8,128)(2,1)} async-done(((bf16[384,1536]{1,0:T(8,128)(2,1)}), bf16[384,24576]{1,0:T(8,128)(2,1)}) %all-gather.2.cloned.1.call-update) | async-done | bytes 18874384 | tf_op jit(solution)/shard_map/all_gather | solution.py:49
  250.6 4.4 %dynamic-slice_convert_fusion = f32[384,3072]{1,0:T(8,128)} fusion(bf16[384,24576]{1,0:T(8,128)(2,1)} %all-gather.2.cloned.1.call-done, s32[]{:T(128)S(6)} %select_n.3), kind=kLoop, calls=%fused_computation.18 | loop fusion | flops 1179648 | bytes 7077892 | tf_op jit(solution)/shard_map/convert_element_type | solution.py:53
  255.0 12.3 %reshape.28 = f32[12,32,96,32]{3,2,1,0:T(8,128)} reshape(f32[384,3072]{1,0:T(8,128)} %dynamic-slice_convert_fusion) | data formatting | bytes 9437184 | tf_op jit(solution)/shard_map/convert_element_type | solution.py:53
  267.3 22.5 %copy.12 = f32[12,32,96,32]{3,2,1,0:T(8,128)} copy(f32[12,32,96,32]{1,2,3,0:T(8,128)} %bitcast.54) | data formatting | bytes 9437184 | tf_op jit(solution)/shard_map/convert_element_type | solution.py:53
  289.7 14.6 %reshape.27 = f32[384,3072]{1,0:T(8,128)} reshape(f32[12,32,96,32]{3,2,1,0:T(8,128)} %copy.12) | data formatting | bytes 9437184 | tf_op jit(solution)/shard_map/convert_element_type | solution.py:53
  304.3 0.0 copy-start.1
  304.3 10.7 %convolution_convert_fusion = bf16[384,1536]{1,0:T(8,128)(2,1)} fusion(bf16[3072,1536]{1,0:T(8,128)(2,1)} %param.5, f32[384,3072]{1,0:T(8,128)} %reshape.27, bf16[2,384,3072]{2,1,0:T(8,128)(2,1)} %param.6), kind=kOutput, calls=%fused_computation.8 | convolution fusion | flops 3628007424 | bytes 17694720 | tf_op jit(solution)/shard_map/dot_general | solution.py:41
  315.0 0.0 all-reduce.5.cloned.1.call-update
  315.1 77.0 %all-reduce.5.cloned.1.call-done = bf16[384,1536]{1,0:T(8,128)(2,1)} async-done(((bf16[384,1536]{1,0:T(8,128)(2,1)}), bf16[384,1536]{1,0:T(8,128)(2,1)}) %all-reduce.5.cloned.1.call-update) | async-done | bytes 1179664 | tf_op jit(solution)/shard_map/psum | solution.py:42
  392.0 0.0 copy-done.1
  392.0 6.1 %fusion.5 = bf16[1,384,1536]{2,1,0:T(8,128)(2,1)S(1)} fusion(bf16[384,1536]{1,0:T(8,128)(2,1)} %all-reduce.5.cloned.1.call-done, bf16[2,384,1536]{2,1,0:T(8,128)(2,1)S(1)} %copy-done.1, f32[2,384,384]{2,1,0:T(8,128)} %param.8), kind=kOutput, calls=%fused_computation.10 | convolution fusion | flops 2723807232 | bytes 6488064 | tf_op jit(solution)/shard_map/dot_general | solution.py:17
  398.1 1.6 pad_maximum_fusion
Async XLA Ops:
  6.5 9.3 %copy-start = (f32[32,32]{1,0:T(8,128)S(1)}, f32[32,32]{1,0:T(8,128)}, u32[]{:S(2)}) copy-start(f32[32,32]{1,0:T(8,128)} %param.9) | copy-start | bytes 12292
  6.5 91.0 %all-reduce.3.cloned.1.call-start = ((), (), s32[]{:S(2)}) async-start(), calls=%async_computation | async-start | bytes 2359296 | tf_op jit(solution)/shard_map/psum | solution.py:42
  15.8 234.8 %all-gather.2.cloned.1.call-start = ((), (), s32[]{:S(2)}) async-start(), calls=%async_computation.1 | async-start | bytes 20054016 | tf_op jit(solution)/shard_map/all_gather | solution.py:49
  131.1 260.9 %all-reduce.5.cloned.1.call-start = ((), (), s32[]{:S(2)}) async-start(), calls=%async_computation.2 | async-start | bytes 2359296 | tf_op jit(solution)/shard_map/psum | solution.py:42
  304.3 87.7 %copy-start.1 = (bf16[2,384,1536]{2,1,0:T(8,128)(2,1)S(1)}, bf16[2,384,1536]{2,1,0:T(8,128)(2,1)}, u32[]{:S(2)}) copy-start(bf16[2,384,1536]{2,1,0:T(8,128)(2,1)} %param.7) | copy-start | bytes 7077892
Sparse Core Ops, SparseCore 0:
  15.9 81.5 all-reduce.2
  131.2 119.3 all-gather.1
  315.2 76.7 all-reduce.4
where the time goes:
time: 407 us; the launch traced here: 406 us
  waiting for transfers between devices  267 us (66%)
  local copies, waits for them, and re-layouts  83.9 us (21%)
  matrix products  32.8 us (8%)
  between operations  13.1 us (3%)
  other arithmetic  9.31 us (2%)
    psum x2, waiting for transfers between devices, advance(): lax.psum(partial_value.astype(jnp.bfloat16), 'past').astype(jnp.float32)  147 us
    all_gather x1, waiting for transfers between devices, per_device(): whole_row = lax.all_gather(energy_one, 'second', axis=1, tiled=True)  119 us
    convert_element_type x3, local copies, waits for them, and re-layouts, per_device(): orbital_flip(gathered, orbitals).astype(jnp.float32)  49.3 us
    dot_general x2, matrix products, advance(): jnp.dot(memory_row, resident, preferred_element_type=jnp.float32)  19.9 us
    dot_general x2, matrix products, solve_front(): jnp.dot(inverse_block, source, precision=lax.Precision.HIGHEST, preferred...  12.9 us
    mul x2, local copies, waits for them, and re-layouts, self_energy(): blocks * pair_coupling[None, :, None, :]  11.2 us
    transpose x1, local copies, waits for them, and re-layouts, orbital_flip(): return blocks.transpose(0, 3, 2, 1).reshape(row_count, col_count)  10.8 us
  transfers between devices with their start and end apart: 3, of which 3 were waited for; matrix products, arithmetic and copies ran while one was open for 3% of the time, Pallas kernels for 0%

commit v1 on v0

--- a/solution.py
+++ b/solution.py
@@ -39,7 +39,9 @@
 
     def advance(memory_row, front_index):
         partial_value = jnp.dot(memory_row, resident, preferred_element_type=jnp.float32)
-        summed = lax.psum(partial_value.astype(jnp.bfloat16), "past").astype(jnp.float32)
+        summed = jnp.sum(lax.all_gather(partial_value.astype(jnp.bfloat16), "past"), axis=0).astype(
+            jnp.float32
+        )
         prior_cols = previous[front_index]
         return solve_front(summed, prior_cols, inverse_part[front_index])
 

time: 407 us -> 658 us (1.62)
  waiting for transfers between devices: 267 us -> 483 us
  local copies, waits for them, and re-layouts: 83.9 us -> 104 us
  other arithmetic: 9.31 us -> 18.9 us
    all_gather x0 -> x2, waiting for transfers between devices: none -> 360 us  [advance(): lax.all_gather(partial_value.astype(jnp.bfloat16), 'past')]
    psum x2 -> x0, waiting for transfers between devices: 147 us -> none  [advance(): lax.psum(partial_value.astype(jnp.bfloat16), 'past').astype(jnp.float32)]
    reshape x1 -> x2, local copies, waits for them, and re-layouts: 7.74 us -> 22.1 us  [orbital_flip(): return blocks.transpose(0, 3, 2, 1).reshape(row_count, col_count)]
    reduce_sum x0 -> x2, other arithmetic: none -> 11.4 us  [advance(): jnp.sum(lax.all_gather(partial_value.astype(jnp.bfloat16), 'past'), axis=0)]
    transpose x1 -> x0, local copies, waits for them, and re-layouts: 10.8 us -> none  [orbital_flip(): return blocks.transpose(0, 3, 2, 1).reshape(row_count, col_count)]
    convert_element_type x3 -> x4, local copies, waits for them, and re-layouts: 49.3 us -> 55.4 us  [per_device(): orbital_flip(gathered, orbitals).astype(jnp.float32)]
    mul x2 -> x3, local copies, waits for them, and re-layouts: 11.2 us -> 13.3 us  [self_energy(): blocks * pair_coupling[None, :, None, :]]
  transfers between devices with their start and end apart: 3 -> 3, of which waited for: 3 -> 3; matrix products, arithmetic and copies ran while one was open for 3% -> 2% of each run, Pallas kernels for 0% -> 0%
where the time goes in v1:
time: 658 us; the launch traced here: 652 us
  waiting for transfers between devices  483 us (73%)
  local copies, waits for them, and re-layouts  104 us (16%)
  matrix products  32.6 us (5%)
  other arithmetic  18.9 us (3%)
  between operations  13.2 us (2%)
    all_gather x2, waiting for transfers between devices, advance(): lax.all_gather(partial_value.astype(jnp.bfloat16), 'past')  360 us
    all_gather x1, waiting for transfers between devices, per_device(): whole_row = lax.all_gather(energy_one, 'second', axis=1, tiled=True)  123 us
    convert_element_type x4, local copies, waits for them, and re-layouts, per_device(): orbital_flip(gathered, orbitals).astype(jnp.float32)  55.4 us
    reshape x2, local copies, waits for them, and re-layouts, orbital_flip(): return blocks.transpose(0, 3, 2, 1).reshape(row_count, col_count)  22.1 us
    dot_general x2, matrix products, advance(): jnp.dot(memory_row, resident, preferred_element_type=jnp.float32)  20 us
    mul x3, local copies, waits for them, and re-layouts, self_energy(): blocks * pair_coupling[None, :, None, :]  13.3 us
  transfers between devices with their start and end apart: 3, of which 3 were waited for; matrix products, arithmetic and copies ran while one was open for 2% of the time, Pallas kernels for 0%

profile of v1, /device:TPU:0, one launch (start us, length us, event | category | flops | bytes accessed | tf_op | source)
XLA Modules:
  0.0 652.0 jit_solution(3939210395595429389)
XLA Ops:
  6.5 0.0 all-gather.8.cloned.1.call-start
  6.5 0.0 copy-start.1
  6.5 9.4 %convolution_convert_fusion.1 = bf16[384,1536]{1,0:T(8,128)(2,1)} fusion(bf16[3072,1536]{1,0:T(8,128)(2,1)} %param.5, bf16[2,384,3072]{2,1,0:T(8,128)(2,1)} %param.6), kind=kOutput, calls=%fused_computation.13 | convolution fusion | flops 3624468480 | bytes 12976128 | tf_op jit(solution)/shard_map/dot_general | solution.py:41
  15.9 0.0 all-gather.8.cloned.1.call-update
  15.9 0.0 all-gather.6.cloned.1.call-start
  16.0 0.0 copy-done.1
  16.0 1.2 fusion.31
  17.2 0.0 copy-start.2
  17.2 0.7 copy.34
  17.9 0.0 copy-done.2
  17.9 4.5 mul.50
  22.4 6.9 %mul.51 = f32[384,1536]{1,0:T(8,128)S(1)} reshape(f32[12,32,48,32]{3,2,1,0:T(8,128)} %mul.50) | data formatting | bytes 4718592 | tf_op jit(solution)/shard_map/mul | solution.py:32
  29.3 2.0 copy.27
  31.3 175.4 %all-gather.8.cloned.1.call-done = bf16[3072,1536]{1,0:T(8,128)(2,1)} async-done(((bf16[384,1536]{1,0:T(8,128)(2,1)}), bf16[3072,1536]{1,0:T(8,128)(2,1)}) %all-gather.8.cloned.1.call-update) | async-done | bytes 9437200 | tf_op jit(solution)/shard_map/all_gather | solution.py:42
  206.6 5.7 reduce_sum.24
  212.3 0.7 copy.22
  213.1 5.7 fusion.3
  218.8 0.6 copy.24
  219.5 4.9 reshape.50
  224.3 13.9 %copy.32 = f32[12,32,48,32]{1,0,3,2:T(8,128)} copy(f32[12,32,48,32]{1,2,3,0:T(8,128)} %bitcast.73) | data formatting | bytes 4718592 | tf_op jit(solution)/shard_map/reshape | solution.py:12
  238.2 8.2 %reshape.59 = f32[384,1536]{0,1:T(8,128)S(1)} reshape(f32[12,32,48,32]{1,0,3,2:T(8,128)} %copy.32) | data formatting | bytes 4718592 | tf_op jit(solution)/shard_map/reshape | solution.py:12
  246.4 3.1 multiply_convert_fusion
  249.5 0.0 all-gather.6.cloned.1.call-update
  249.5 0.0 all-gather.10.cloned.1.call-start
  249.5 123.1 %all-gather.6.cloned.1.call-done = bf16[384,24576]{0,1:T(8,128)(2,1)} async-done(((bf16[384,1536]{0,1:T(8,128)(2,1)}), bf16[384,24576]{0,1:T(8,128)(2,1)}) %all-gather.6.cloned.1.call-update) | async-done | bytes 18874384 | tf_op jit(solution)/shard_map/all_gather | solution.py:51
  372.6 4.1 dynamic-slice_convert_fusion
  376.8 6.0 copy.28
  382.8 12.3 %reshape.56 = f32[12,32,96,32]{3,2,1,0:T(8,128)} reshape(f32[384,3072]{1,0:T(8,128)} %copy.28) | data formatting | bytes 9437184 | tf_op jit(solution)/shard_map/convert_element_type | solution.py:55
  395.1 22.5 %copy.29 = f32[12,32,96,32]{3,2,1,0:T(8,128)} copy(f32[12,32,96,32]{1,2,3,0:T(8,128)} %bitcast.72) | data formatting | bytes 9437184 | tf_op jit(solution)/shard_map/convert_element_type | solution.py:55
  417.6 14.6 %reshape.55 = f32[384,3072]{1,0:T(8,128)} reshape(f32[12,32,96,32]{3,2,1,0:T(8,128)} %copy.29) | data formatting | bytes 9437184 | tf_op jit(solution)/shard_map/convert_element_type | solution.py:55
  432.2 0.0 copy-start
  432.2 10.7 %convolution_convert_fusion = bf16[384,1536]{1,0:T(8,128)(2,1)} fusion(bf16[3072,1536]{1,0:T(8,128)(2,1)} %param.5, f32[384,3072]{1,0:T(8,128)} %reshape.55, bf16[2,384,3072]{2,1,0:T(8,128)(2,1)} %param.6), kind=kOutput, calls=%fused_computation.12 | convolution fusion | flops 3628007424 | bytes 17694720 | tf_op jit(solution)/shard_map/dot_general | solution.py:41
  442.8 0.0 all-gather.10.cloned.1.call-update
  442.8 0.0 copy-done
  442.9 0.7 copy.35
  443.6 185.0 %all-gather.10.cloned.1.call-done = bf16[3072,1536]{1,0:T(8,128)(2,1)} async-done(((bf16[384,1536]{1,0:T(8,128)(2,1)}), bf16[3072,1536]{1,0:T(8,128)(2,1)}) %all-gather.10.cloned.1.call-update) | async-done | bytes 9437200 | tf_op jit(solution)/shard_map/all_gather | solution.py:42
  628.6 5.7 reduce_sum.25
  634.3 1.4 copy.30
  635.7 6.8 %fusion.5 = bf16[1,384,1536]{1,2,0:T(8,128)(2,1)S(1)} fusion(bf16[1,384,1536]{1,2,0:T(8,128)(2,1)S(1)} %copy.35, bf16[384,1536]{0,1:T(8,128)(2,1)} %copy.30, f32[2,384,384]{2,1,0:T(8,128)} %param.8), kind=kOutput, calls=%fused_computation.14 | convolution fusion | flops 2723807232 | bytes 6488064 | tf_op jit(solution)/shard_map/dot_general | solution.py:17
  642.6 0.3 pad_maximum_fusion
  642.9 2.6 copy.31
Async XLA Ops:
  6.5 200.1 %all-gather.8.cloned.1.call-start = ((), (), s32[]{:S(2)}) async-start(), calls=%async_computation.1 | async-start | bytes 10616832 | tf_op jit(solution)/shard_map/all_gather | solution.py:42
  6.5 9.4 %copy-start.1 = (bf16[2,384,1536]{2,1,0:T(8,128)(2,1)S(1)}, bf16[2,384,1536]{2,1,0:T(8,128)(2,1)}, u32[]{:S(2)}) copy-start(bf16[2,384,1536]{2,1,0:T(8,128)(2,1)} %param.7) | copy-start | bytes 7077892
  15.9 356.7 %all-gather.6.cloned.1.call-start = ((), (), s32[]{:S(2)}) async-start(), calls=%async_computation | async-start | bytes 20054016 | tf_op jit(solution)/shard_map/all_gather | solution.py:51
  17.2 0.7 copy-start.2
  249.5 379.1 %all-gather.10.cloned.1.call-start = ((), (), s32[]{:S(2)}) async-start(), calls=%async_computation.2 | async-start | bytes 10616832 | tf_op jit(solution)/shard_map/all_gather | solution.py:42
  432.2 10.7 %copy-start = (bf16[1,384,1536]{2,1,0:T(8,128)(2,1)S(1)}, bf16[1,384,1536]{2,1,0:T(8,128)(2,1)}, u32[]{:S(2)}) copy-start(bf16[1,384,1536]{2,1,0:T(8,128)(2,1)} %get-tuple-element.6) | copy-start | bytes 3538948
Sparse Core Ops, SparseCore 0:
  16.0 190.5 all-gather.7
  249.6 122.9 all-gather.5
  443.0 185.5 all-gather.9

commit v2 on v0

--- a/solution.py
+++ b/solution.py
@@ -46,7 +46,9 @@
     front_one = advance(memory[0], 0)
     energy_one = self_energy(front_one, pair_coupling)
     span_cols = memory.shape[2]
-    whole_row = lax.all_gather(energy_one, "second", axis=1, tiled=True)
+    whole_row = jnp.concatenate(
+        lax.all_to_all(jnp.stack([energy_one] * lax.axis_size("second")), "second", 0, 0), axis=1
+    )
     gathered = lax.dynamic_slice_in_dim(whole_row, lax.axis_index("past") * span_cols, span_cols, 1)
     orbitals = pair_coupling.shape[0]
     memory_next = (

time: 407 us -> 619 us (1.52)
  waiting for transfers between devices: 267 us -> 457 us
  local copies, waits for them, and re-layouts: 83.9 us -> 98.6 us
  starting transfers between devices: 0.27 us -> 6.77 us
    all_to_all x0 -> x1, waiting for transfers between devices: none -> 306 us  [per_device(): lax.all_to_all(jnp.stack([energy_one] * lax.axis_size('second')), 'second...]
    all_gather x1 -> x0, waiting for transfers between devices: 119 us -> none  [per_device(): whole_row = lax.all_gather(energy_one, 'second', axis=1, tiled=True)]
    another operation x0 -> x1, local copies, waits for them, and re-layouts: none -> 6.94 us  [per_device(): jnp.stack([energy_one] * lax.axis_size('second'))]
    all_to_all x0 -> x1, starting transfers between devices: none -> 6.72 us  [per_device(): lax.all_to_all(jnp.stack([energy_one] * lax.axis_size('second')), 'second...]
    convert_element_type x3 -> x4, local copies, waits for them, and re-layouts: 49.3 us -> 55.4 us  [per_device(): orbital_flip(gathered, orbitals).astype(jnp.float32)]
  transfers between devices with their start and end apart: 3 -> 3, of which waited for: 3 -> 3; matrix products, arithmetic and copies ran while one was open for 3% -> 2% of each run, Pallas kernels for 0% -> 0%
where the time goes in v2:
time: 619 us; the launch traced here: 617 us
  waiting for transfers between devices  457 us (74%)
  local copies, waits for them, and re-layouts  98.6 us (16%)
  matrix products  32.8 us (5%)
  between operations  13.5 us (2%)
  other arithmetic  9.04 us (1%)
  starting transfers between devices  6.77 us (1%)
    all_to_all x1, waiting for transfers between devices, per_device(): lax.all_to_all(jnp.stack([energy_one] * lax.axis_size('second')), 'second...  306 us
    psum x2, waiting for transfers between devices, advance(): lax.psum(partial_value.astype(jnp.bfloat16), 'past').astype(jnp.float32)  150 us
    convert_element_type x4, local copies, waits for them, and re-layouts, per_device(): orbital_flip(gathered, orbitals).astype(jnp.float32)  55.4 us
    dot_general x2, matrix products, advance(): jnp.dot(memory_row, resident, preferred_element_type=jnp.float32)  19.9 us
    dot_general x2, matrix products, solve_front(): jnp.dot(inverse_block, source, precision=lax.Precision.HIGHEST, preferred...  12.9 us
  transfers between devices with their start and end apart: 3, of which 3 were waited for; matrix products, arithmetic and copies ran while one was open for 2% of the time, Pallas kernels for 0%

profile of v2, /device:TPU:0, one launch (start us, length us, event | category | flops | bytes accessed | tf_op | source)
XLA Modules:
  0.0 617.2 jit_solution(13687921291772841776)
XLA Ops:
  6.5 0.0 copy-start
  6.5 0.0 all-reduce.3.cloned.1.call-start
  6.5 9.2 %convolution_convert_fusion.1 = bf16[384,1536]{1,0:T(8,128)(2,1)} fusion(bf16[3072,1536]{1,0:T(8,128)(2,1)} %param.5, bf16[2,384,3072]{2,1,0:T(8,128)(2,1)} %param.6), kind=kOutput, calls=%fused_computation.9 | convolution fusion | flops 3624468480 | bytes 12976128 | tf_op jit(solution)/shard_map/dot_general | solution.py:41
  15.8 0.0 all-reduce.3.cloned.1.call-update
  15.8 0.0 copy-done
  15.8 4.4 mul.29
  20.2 6.7 %mul.30 = f32[384,1536]{1,0:T(8,128)S(1)} reshape(f32[12,32,48,32]{3,2,1,0:T(8,128)} %mul.29) | data formatting | bytes 4718592 | tf_op jit(solution)/shard_map/mul | solution.py:32
  27.0 70.6 %all-reduce.3.cloned.1.call-done = bf16[384,1536]{1,0:T(8,128)(2,1)} async-done(((bf16[384,1536]{1,0:T(8,128)(2,1)}), bf16[384,1536]{1,0:T(8,128)(2,1)}) %all-reduce.3.cloned.1.call-update) | async-done | bytes 1179664 | tf_op jit(solution)/shard_map/psum | solution.py:42
  97.5 6.8 %fusion.3 = bf16[384,1536]{1,0:T(8,128)(2,1)S(1)} fusion(bf16[384,1536]{1,0:T(8,128)(2,1)} %all-reduce.3.cloned.1.call-done, bf16[2,384,1536]{2,1,0:T(8,128)(2,1)} %param.7, f32[2,384,384]{2,1,0:T(8,128)} %param.8), kind=kOutput, calls=%fused_computation.6 | convolution fusion | flops 2723807232 | bytes 6488064 | tf_op jit(solution)/shard_map/dot_general | solution.py:17
  104.3 4.9 reshape.30
  109.2 10.8 %copy.10 = f32[12,32,48,32]{3,2,1,0:T(8,128)} copy(f32[12,32,48,32]{1,2,3,0:T(8,128)} %bitcast.58) | data formatting | bytes 4718592 | tf_op jit(solution)/shard_map/transpose | solution.py:12
  120.0 7.7 %reshape.31 = f32[384,1536]{1,0:T(8,128)} reshape(f32[12,32,48,32]{3,2,1,0:T(8,128)} %copy.10) | data formatting | bytes 4718592 | tf_op jit(solution)/shard_map/reshape | solution.py:12
  127.7 3.3 multiply_convert_fusion
  131.0 1.7 copy.11
  132.7 6.9 %stack.9 = bf16[16,384,1536]{1,2,0:T(8,128)(2,1)} broadcast(bf16[384,1536]{0,1:T(8,128)(2,1)S(1)} %copy.11), dimensions={1,2} | broadcast | bytes 20054016 | tf_op jit(solution)/shard_map/stack | solution.py:50
  139.7 6.7 %all-to-all-start = ((bf16[16,384,1536]{1,2,0:T(8,128)(2,1)}), bf16[16,384,1536]{1,2,0:T(8,128)(2,1)}, u32[]{:S(2)}, u32[]{:S(2)}) async-start(bf16[16,384,1536]{1,2,0:T(8,128)(2,1)} %stack.9), calls=%async_computation | async-start | bytes 37748736 | tf_op jit(solution)/shard_map/all_to_all | solution.py:50
  146.4 0.0 all-reduce.5.cloned.1.call-start
  146.5 306.4 %all-to-all-done = bf16[16,384,1536]{1,2,0:T(8,128)(2,1)} async-done(((bf16[16,384,1536]{1,2,0:T(8,128)(2,1)}), bf16[16,384,1536]{1,2,0:T(8,128)(2,1)}, u32[]{:S(2)}, u32[]{:S(2)}) %all-to-all-start) | async-done | bytes 18874400 | tf_op jit(solution)/shard_map/all_to_all | solution.py:50
  452.8 4.1 dynamic-slice_convert_fusion
  457.0 6.0 copy.12
  463.0 12.3 %reshape.38 = f32[12,32,96,32]{3,2,1,0:T(8,128)} reshape(f32[384,3072]{1,0:T(8,128)} %copy.12) | data formatting | bytes 9437184 | tf_op jit(solution)/shard_map/convert_element_type | solution.py:55
  475.3 22.5 %copy.13 = f32[12,32,96,32]{3,2,1,0:T(8,128)} copy(f32[12,32,96,32]{1,2,3,0:T(8,128)} %bitcast.57) | data formatting | bytes 9437184 | tf_op jit(solution)/shard_map/convert_element_type | solution.py:55
  497.8 14.6 %reshape.37 = f32[384,3072]{1,0:T(8,128)} reshape(f32[12,32,96,32]{3,2,1,0:T(8,128)} %copy.13) | data formatting | bytes 9437184 | tf_op jit(solution)/shard_map/convert_element_type | solution.py:55
  512.4 0.0 copy-start.1
  512.4 10.7 %convolution_convert_fusion = bf16[384,1536]{1,0:T(8,128)(2,1)} fusion(bf16[3072,1536]{1,0:T(8,128)(2,1)} %param.5, f32[384,3072]{1,0:T(8,128)} %reshape.37, bf16[2,384,3072]{2,1,0:T(8,128)(2,1)} %param.6), kind=kOutput, calls=%fused_computation.8 | convolution fusion | flops 3628007424 | bytes 17694720 | tf_op jit(solution)/shard_map/dot_general | solution.py:41
  523.1 0.0 all-reduce.5.cloned.1.call-update
  523.1 79.6 %all-reduce.5.cloned.1.call-done = bf16[384,1536]{1,0:T(8,128)(2,1)} async-done(((bf16[384,1536]{1,0:T(8,128)(2,1)}), bf16[384,1536]{1,0:T(8,128)(2,1)}) %all-reduce.5.cloned.1.call-update) | async-done | bytes 1179664 | tf_op jit(solution)/shard_map/psum | solution.py:42
  602.7 0.0 copy-done.1
  602.7 6.1 fusion.5
  608.7 1.6 pad_maximum_fusion
Async XLA Ops:
  6.5 9.3 %copy-start = (f32[32,32]{1,0:T(8,128)S(1)}, f32[32,32]{1,0:T(8,128)}, u32[]{:S(2)}) copy-start(f32[32,32]{1,0:T(8,128)} %param.9) | copy-start | bytes 12292
  6.5 91.0 %all-reduce.3.cloned.1.call-start = ((), (), s32[]{:S(2)}) async-start(), calls=%async_computation.1 | async-start | bytes 2359296 | tf_op jit(solution)/shard_map/psum | solution.py:42
  139.7 313.2 %all-to-all-start = ((bf16[16,384,1536]{1,2,0:T(8,128)(2,1)}), bf16[16,384,1536]{1,2,0:T(8,128)(2,1)}, u32[]{:S(2)}, u32[]{:S(2)}) async-start(bf16[16,384,1536]{1,2,0:T(8,128)(2,1)} %stack.9), calls=%async_computation | async-start | bytes 37748736 | tf_op jit(solution)/shard_map/all_to_all | solution.py:50
  146.4 456.2 %all-reduce.5.cloned.1.call-start = ((), (), s32[]{:S(2)}) async-start(), calls=%async_computation.2 | async-start | bytes 2359296 | tf_op jit(solution)/shard_map/psum | solution.py:42
  512.4 90.3 %copy-start.1 = (bf16[2,384,1536]{2,1,0:T(8,128)(2,1)S(1)}, bf16[2,384,1536]{2,1,0:T(8,128)(2,1)}, u32[]{:S(2)}) copy-start(bf16[2,384,1536]{2,1,0:T(8,128)(2,1)} %param.7) | copy-start | bytes 7077892
Sparse Core Ops, SparseCore 0:
  15.9 81.5 all-reduce.2
  523.2 79.3 all-reduce.4
